TPU v7x, 128 devices: a whole 4x4x4 slice. The times are simulated.
128 devices in a mesh: img: 16 (over z_lo, x, core), head: 2 (over z_hi), txt: 4 (over y).
Axes of the slice: x: 4, y: 4, z: 4 (z_hi: 2, z_lo: 2; z = z_hi * 2 + z_lo), core: 2. Of those that a mesh axis runs over, the one named last changes fastest.
Arguments:
- image_feats: bfloat16 [16384, 7680], P(('img', 'txt'), 'head'), may hold values from -6 to 6
- key_weight: bfloat16 [7680, 512], P('head'), may hold values from -0.0625 to 0.0625
- value_weight: bfloat16 [7680, 512], P('head'), may hold values from -0.0625 to 0.0625
- queries: bfloat16 [1024, 4096], P('txt', 'head'), may hold values from -21 to 21
- grad_out: bfloat16 [1024, 4096], P('txt', 'head'), may hold values from -768 to 768
- tile_image: int32 [128], P('img'), may hold values from 0 to 7, never falling along the last dimension, each value on 1 to 32 neighbouring positions
- text_sees: int32 [8, 8], replicated, may hold values from 0 to 1, as said below
Outputs:
- attn_out: bfloat16 [1024, 4096], P('txt', 'head')
- grad_feats: bfloat16 [16384, 7680], P(('img', 'txt'), 'head')
Inputs may be any that keep to these rules, and one draw needn't show every extreme that they name: `text_sees`: every row holds at least one 1.
All inputs are finite; a program needn't handle non-finite values.
Results may differ from a plain program's by a relative error of at most 0.012.
The roundings to bfloat16 on the way count: a program that leaves them out, or rounds other values in their place, can miss the bound.
Values may be sent and summed in bfloat16 or wider, within the bound.
No kernel may reach another device: no remote copies, remote signals or barrier semaphores. Data moves between devices by JAX's collectives and lax.ppermute only.
A program may use at most 128 MiB of HBM per device.

v0:
```python
import math
import jax
import jax.numpy as jnp
from jax import lax
from jax.sharding import PartitionSpec as P

HD = 128
TILE = 128
TBLK = 128


def in_blocks(array, dim, length):
    before, after = (array.shape[:dim], array.shape[dim + 1 :])
    return jnp.moveaxis(array.reshape(*before, length, -1, *after), dim, 0)


def summed_on_arrival(array, axis, dim):
    length = lax.axis_size(axis)
    blocks = lax.all_to_all(in_blocks(array, dim, length), axis, 0, 0, tiled=True)
    return jnp.sum(blocks, axis=0)


def in_one_piece(arrays, axis, dim, along):
    ends, at = ([], 0)
    for a in arrays[:-1]:
        at += a.shape[along]
        ends.append(at)
    both = jnp.concatenate(arrays, axis=along)
    return tuple(jnp.split(summed_on_arrival(both, axis, dim), ends, axis=along))


def sent_to_all(array, axis):
    copies = jnp.broadcast_to(array, (lax.axis_size(axis), *array.shape))
    return lax.all_to_all(copies, axis, split_axis=0, concat_axis=0, tiled=True)


def of_everyone(array, axis):
    everything = sent_to_all(array, axis)
    return jnp.max(everything, axis=0)


def of_everyone_2(array, axis):
    everything = sent_to_all(array, axis)
    return jnp.sum(everything, axis=0)


def joined_along(blocks, dim):
    blocks = jnp.moveaxis(blocks, 0, dim)
    shape = blocks.shape
    return blocks.reshape(*shape[:dim], shape[dim] * shape[dim + 1], *shape[dim + 2 :])


def gather_directly(array, axis, dim):
    return joined_along(sent_to_all(array, axis), dim)


def side_by_side(arrays, axis, dim, along):
    widths = [a.shape[along] for a in arrays]
    both = jnp.concatenate(arrays, axis=along)
    out = lax.all_gather(both, axis, axis=dim, tiled=True)
    return tuple(jnp.split(out, [sum(widths[:k]) for k in range(1, len(widths))], axis=along))


def build_mask(text_sees, tile_image, text_count):
    blocks_total = text_sees.shape[0]
    images_total = text_sees.shape[1]
    text_rows = lax.axis_index("txt") * text_count + jnp.arange(text_count, dtype=jnp.int32)
    text_block = text_rows // TBLK
    block_onehot = (
        text_block[:, None] == jnp.arange(blocks_total, dtype=jnp.int32)[None, :]
    ).astype(jnp.float32)
    row_sees = jnp.dot(block_onehot, text_sees.astype(jnp.float32))
    tile_onehot = (
        tile_image[:, None] == jnp.arange(images_total, dtype=jnp.int32)[None, :]
    ).astype(jnp.float32)
    tile_allowed = jnp.dot(row_sees, tile_onehot.T) > 0.5
    return jnp.repeat(tile_allowed, TILE, axis=1)


def shards(image_feats, key_weight, value_weight, queries, grad_out, tile_image, text_sees):
    key_part = jnp.dot(image_feats, key_weight, preferred_element_type=jnp.float32)
    value_part = jnp.dot(image_feats, value_weight, preferred_element_type=jnp.float32)
    key_own, value_own = in_one_piece((key_part, value_part), "head", 1, 0)
    keys, values = (
        lax.all_gather(key_own.astype(jnp.bfloat16), "txt", axis=0, tiled=True),
        lax.all_gather(value_own.astype(jnp.bfloat16), "txt", axis=0, tiled=True),
    )
    text_count = queries.shape[0]
    key_count = keys.shape[0]
    groups = keys.shape[1] // HD
    repeats = queries.shape[1] // (groups * HD)
    scale_factor = 1.0 / math.sqrt(HD)
    allowed = build_mask(text_sees, tile_image, text_count)
    query_heads = queries.reshape(text_count, groups, repeats, HD)
    grad_heads = grad_out.reshape(text_count, groups, repeats, HD)
    key_heads = keys.reshape(key_count, groups, HD)
    value_heads = values.reshape(key_count, groups, HD)
    scores = (
        jnp.einsum("tgrd,jgd->grtj", query_heads, key_heads, preferred_element_type=jnp.float32)
        * scale_factor
    )
    masked = jnp.where(allowed[None, None], scores, -1e30)
    row_max = of_everyone(jnp.max(masked, axis=-1), "img")
    weights = jnp.exp(masked - row_max[..., None]).astype(jnp.bfloat16)
    local_totals = (
        jnp.sum(weights, axis=-1, dtype=jnp.float32)
        .transpose(2, 0, 1)
        .reshape(text_count, groups * repeats)
    )
    numerator = jnp.einsum(
        "grtj,jgd->tgrd", weights, value_heads, preferred_element_type=jnp.float32
    )
    numerator = numerator.reshape(text_count, groups * repeats, HD)
    num_rows = summed_on_arrival(numerator, "img", 0)
    totals = of_everyone_2(local_totals, "img")
    share_rows = num_rows.shape[0]
    row_totals = lax.dynamic_slice_in_dim(totals, lax.axis_index("img") * share_rows, share_rows, 0)
    out_rows = (
        (num_rows / row_totals[..., None])
        .astype(jnp.bfloat16)
        .reshape(share_rows, groups * repeats * HD)
    )
    attn_out = gather_directly(out_rows, "img", 0)
    log_total = row_max + jnp.log(totals.reshape(text_count, groups, repeats).transpose(1, 2, 0))
    products = grad_out.astype(jnp.float32) * attn_out.astype(jnp.float32)
    row_delta = jnp.sum(products.reshape(text_count, groups, repeats, HD), axis=-1).transpose(
        1, 2, 0
    )
    key_grads = []
    value_grads = []
    for group_index in range(groups):
        probabilities = jnp.exp(masked[group_index] - log_total[group_index][..., None])
        grad_probs = jnp.einsum(
            "trd,jd->rtj",
            grad_heads[:, group_index],
            value_heads[:, group_index],
            preferred_element_type=jnp.float32,
        )
        grad_scores = (
            probabilities * (grad_probs - row_delta[group_index][..., None]) * scale_factor
        ).astype(jnp.bfloat16)
        value_grads.append(
            jnp.einsum(
                "rtj,trd->jd",
                probabilities.astype(jnp.bfloat16),
                grad_heads[:, group_index],
                preferred_element_type=jnp.float32,
            )
        )
        key_grads.append(
            jnp.einsum(
                "rtj,trd->jd",
                grad_scores,
                query_heads[:, group_index],
                preferred_element_type=jnp.float32,
            )
        )
    key_grad = jnp.concatenate(key_grads, axis=1)
    value_grad = jnp.concatenate(value_grads, axis=1)
    key_own_grad, value_own_grad = in_one_piece((key_grad, value_grad), "txt", 0, 1)
    key_all, value_all = side_by_side(
        (key_own_grad.astype(jnp.bfloat16), value_own_grad.astype(jnp.bfloat16)), "head", 1, 0
    )
    contract = (((1,), (1,)), ((), ()))
    grad_feats = lax.dot_general(key_all, key_weight, contract, preferred_element_type=jnp.float32)
    grad_feats = grad_feats + lax.dot_general(
        value_all, value_weight, contract, preferred_element_type=jnp.float32
    )
    return (attn_out, grad_feats.astype(jnp.bfloat16))


def solution(mesh):
    placed = (
        P(("img", "txt"), "head"),
        P("head", None),
        P("head", None),
        P("txt", "head"),
        P("txt", "head"),
        P("img"),
        P(),
    )
    return jax.shard_map(
        shards,
        mesh=mesh,
        in_specs=placed,
        out_specs=(P("txt", "head"), P(("img", "txt"), "head")),
        check_vma=False,
    )
```

profile of v0, /device:TPU:0, one launch (start us, length us, event | category | flops | bytes accessed | tf_op | source)
XLA Modules:
  0.0 227.6 jit_solution(16640007711787524154)
XLA Ops:
  0.6 0.0 copy-start
  0.6 0.0 copy-start.3
  0.7 1.5 copy-done
  2.2 3.5 %fusion.59 = f32[256,512]{1,0:T(8,128)S(1)} fusion(bf16[256,3840]{1,0:T(8,128)(2,1)S(1)} %copy-done, bf16[3840,512]{1,0:T(8,128)(2,1)} %param.8), kind=kOutput, calls=%fused_computation.72 | convolution fusion | flops 1006632960 | bytes 6422528 | tf_op jit(solution)/shard_map/dot_general | solution.py:81
  5.7 0.0 copy-done.3
  5.7 1.2 fusion.60
  6.8 0.0 copy-start.7
  6.9 0.0 copy-start.8
  6.9 0.1 pad_maximum_fusion.1
  7.0 1.1 copy.131
  8.0 5.2 %all-to-all-start = ((f32[2,512,256]{2,1,0:T(8,128)}), f32[2,512,256]{2,1,0:T(8,128)S(1)}, u32[]{:S(2)}, u32[]{:S(2)}) async-start(f32[2,512,256]{2,1,0:T(8,128)} %bitcast.154), calls=%async_computation | async-start | bytes 2097152 | tf_op jit(solution)/shard_map/all_to_all | solution.py:19
  13.2 1.5 copy.82
  14.7 0.0 copy-done.7
  14.8 0.3 fusion.42
  15.1 13.2 %all-to-all-done = f32[2,512,256]{2,1,0:T(8,128)S(1)} async-done(((f32[2,512,256]{2,1,0:T(8,128)}), f32[2,512,256]{2,1,0:T(8,128)S(1)}, u32[]{:S(2)}, u32[]{:S(2)}) %all-to-all-start) | async-done | bytes 1048608 | tf_op jit(solution)/shard_map/all_to_all | solution.py:19
  28.3 0.1 reduce_sum.54
  28.4 13.9 %all_gather.10 = bf16[1024,256]{1,0:T(8,128)(2,1)S(1)} all-gather(bf16[256,256]{1,0:T(8,128)(2,1)S(1)} %get-tuple-element.6), channel_id=1, replica_groups=mesh['img'=16,'head'=2,'txt'=4] {'txt'}, dimensions={0}, use_global_device_ids=true | all-gather | bytes 655360 | tf_op jit(solution)/shard_map/all_gather | solution.py:85
  42.3 0.2 copy.81
  42.5 0.1 broadcast_in_dim.32
  42.6 7.3 %fusion.58 = (f32[2,8,256]{2,1,0:T(8,128)S(1)}, f32[2,8,256,1024]{2,3,1,0:T(8,128)}) fusion(bf16[1024,2,128,1]{0,2,3,1:T(8,128)(2,1)S(1)} %bitcast.166, bf16[256,2,8,128]{0,3,2,1:T(8,128)(2,1)S(1)} %bitcast.161, pred[256,1024]{0,1:T(8,128)(4,1)S(1)} %bitcast.164), kind=kOutput, calls=%fused_computation.71 | convolution fusion | flops 1086320640 | bytes 18628608 | tf_op jit(solution)/shard_map/tgrd,jgd->grtj/dot_general | solution.py:99
  49.9 0.7 broadcast_in_dim.36
  50.6 4.9 %all-to-all-start.1 = ((f32[16,2,8,256]{3,2,1,0:T(8,128)}), f32[16,2,8,256]{3,2,1,0:T(8,128)S(1)}, u32[]{:S(2)}, u32[]{:S(2)}) async-start(f32[16,2,8,256]{3,2,1,0:T(8,128)} %broadcast_in_dim.36), calls=%async_computation.1 | async-start | bytes 524288 | tf_op jit(solution)/shard_map/all_to_all | solution.py:34
  55.4 12.9 %all_gather.9 = bf16[1024,256]{1,0:T(8,128)(2,1)S(1)} all-gather(bf16[256,256]{1,0:T(8,128)(2,1)S(1)} %get-tuple-element.7), channel_id=1, replica_groups=mesh['img'=16,'head'=2,'txt'=4] {'txt'}, dimensions={0}, use_global_device_ids=true | all-gather | bytes 655360 | tf_op jit(solution)/shard_map/all_gather | solution.py:86
  68.4 0.2 copy.80
  68.6 0.0 all-to-all-done.1
  68.6 8.0 %convert_reduce_fusion = f32[2,8,256]{2,1,0:T(8,128)S(1)} fusion(f32[2,8,256,1024]{2,3,1,0:T(8,128)} %get-tuple-element.11, f32[2,8,256]{2,1,0:T(8,128)S(1)} %reduce_max.19), kind=kLoop, calls=%fused_computation.1 | loop fusion | flops 16773120 | bytes 16809984 | tf_op jit(solution)/shard_map/reduce_sum | solution.py:106
  76.6 0.7 broadcast_in_dim.37
  77.3 5.5 %all-to-all-start.3 = ((f32[16,256,16]{1,2,0:T(8,128)}), f32[16,256,16]{1,2,0:T(8,128)S(1)}, u32[]{:S(2)}, u32[]{:S(2)}) async-start(f32[16,256,16]{1,2,0:T(8,128)} %broadcast_in_dim.37), calls=%async_computation.3 | async-start | bytes 524288 | tf_op jit(solution)/shard_map/all_to_all | solution.py:34
  82.9 10.0 %fusion.26 = f32[256,2,8,128]{0,3,2,1:T(8,128)} fusion(bf16[1024,2,128,1]{0,2,3,1:T(8,128)(2,1)S(1)} %bitcast.167, f32[2,8,256,1024]{2,3,1,0:T(8,128)} %get-tuple-element.11, f32[2,8,256]{2,1,0:T(8,128)S(1)} %reduce_max.19), kind=kOutput, calls=%fused_computation.31 | convolution fusion | flops 1082130432 | bytes 19415040 | tf_op jit(solution)/shard_map/grtj,jgd->tgrd/dot_general | solution.py:110
  92.9 3.2 %copy.86 = f32[256,2,8,128]{3,2,1,0:T(8,128)} copy(f32[256,2,8,128]{0,3,2,1:T(8,128)} %fusion.26) | data formatting | bytes 4194304 | tf_op jit(solution)/shard_map/grtj,jgd->tgrd/transpose | solution.py:110
  96.1 0.0 all-to-all-done.3
  96.1 5.8 %all-to-all-start.2 = ((f32[16,16,16,128]{3,2,1,0:T(8,128)}), f32[16,16,16,128]{3,2,1,0:T(8,128)}, u32[]{:S(2)}, u32[]{:S(2)}) async-start(f32[16,16,16,128]{3,2,1,0:T(8,128)} %bitcast.158), calls=%async_computation.2 | async-start | bytes 4194304 | tf_op jit(solution)/shard_map/all_to_all | solution.py:19
  101.9 0.0 copy-done.2
  101.9 1.3 copy.88
  103.2 0.1 constant_dynamic-slice_fusion
  103.3 0.1 copy.87
  103.4 26.6 %all-to-all-done.2 = f32[16,16,16,128]{3,2,1,0:T(8,128)} async-done(((f32[16,16,16,128]{3,2,1,0:T(8,128)}), f32[16,16,16,128]{3,2,1,0:T(8,128)}, u32[]{:S(2)}, u32[]{:S(2)}) %all-to-all-start.2) | async-done | bytes 2097184 | tf_op jit(solution)/shard_map/all_to_all | solution.py:19
  130.0 1.7 reduce_sum.55
  131.7 0.1 divide_convert_fusion
  131.9 1.1 broadcast_in_dim.38
  132.9 4.6 %all-to-all-start.4 = ((bf16[16,16,2048]{2,1,0:T(8,128)(2,1)}), bf16[16,16,2048]{2,1,0:T(8,128)(2,1)S(1)}, u32[]{:S(2)}, u32[]{:S(2)}) async-start(bf16[16,16,2048]{2,1,0:T(8,128)(2,1)} %broadcast_in_dim.38), calls=%async_computation.4 | async-start | bytes 2097152 | tf_op jit(solution)/shard_map/all_to_all | solution.py:34
  137.5 0.0 copy-start.5
  137.5 5.9 %fusion.33 = f32[1024,128]{0,1:T(8,128)} fusion(f32[2,8,256,1024]{2,3,1,0:T(8,128)} %get-tuple-element.11, f32[8,256]{1,0:T(8,128)S(1)} %get-tuple-element.8, bf16[256,2,8,128]{0,3,2,1:T(8,128)(2,1)} %bitcast.171), kind=kOutput, calls=%fused_computation.34 | convolution fusion | flops 541065216 | bytes 9445376 | tf_op jit(solution)/shard_map/rtj,trd->jd/dot_general | solution.py:143
  143.4 5.7 %fusion.36 = f32[1024,128]{0,1:T(8,128)} fusion(f32[2,8,256,1024]{2,3,1,0:T(8,128)} %get-tuple-element.11, f32[8,256]{1,0:T(8,128)S(1)} %get-tuple-element.9, bf16[256,2,8,128]{0,3,2,1:T(8,128)(2,1)S(1)} %bitcast.174), kind=kOutput, calls=%fused_computation.35 | convolution fusion | flops 541065216 | bytes 9445376 | tf_op jit(solution)/shard_map/rtj,trd->jd/dot_general | solution.py:143
  149.1 4.9 %all-to-all-done.4 = bf16[16,16,2048]{2,1,0:T(8,128)(2,1)S(1)} async-done(((bf16[16,16,2048]{2,1,0:T(8,128)(2,1)}), bf16[16,16,2048]{2,1,0:T(8,128)(2,1)S(1)}, u32[]{:S(2)}, u32[]{:S(2)}) %all-to-all-start.4) | async-done | bytes 1048608 | tf_op jit(solution)/shard_map/all_to_all | solution.py:34
  154.0 1.6 multiply_bitcast_fusion
  155.6 1.7 copy.126
  157.3 2.4 %reduce_sum.58 = f32[256,2,8]{2,1,0:T(2,128)S(1)} reduce(f32[256,2,8,128]{3,2,1,0:T(8,128)} %bitcast.157, f32[]{:T(128)} %constant.14.clone.1), dimensions={3}, to_apply=%region_6.7 | reduce | flops 520192 | bytes 2113540 | tf_op jit(solution)/shard_map/reduce_sum | solution.py:126
  159.7 0.2 fusion.56
  159.9 0.1 copy.91
  159.9 0.1 copy.95
  160.0 7.6 %fusion.30 = f32[1024,128]{0,1:T(8,128)} fusion(f32[2,8,256,1024]{2,3,1,0:T(8,128)} %get-tuple-element.11, f32[8,256]{1,0:T(8,128)S(1)} %copy.91, f32[8,256]{1,0:T(8,128)S(1)} %get-tuple-element.8, bf16[256,2,8,128]{0,3,2,1:T(8,128)(2,1)S(1)} %bitcast.162, bf16[256,2,8,128]{0,3,2,1:T(8,128)(2,1)} %bitcast.172, bf16[1024,2,128]{0,2,1:T(8,128)(2,1)S(1)} %bitcast.168), kind=kOutput, calls=%fused_computation.33 | convolution fusion | flops 1084227584 | bytes 10240000 | tf_op jit(solution)/shard_map/rtj,trd->jd/dot_general | solution.py:151
  167.5 7.6 %fusion.27 = f32[1024,128]{0,1:T(8,128)} fusion(f32[2,8,256,1024]{2,3,1,0:T(8,128)} %get-tuple-element.11, f32[8,256]{1,0:T(8,128)S(1)} %copy.95, f32[8,256]{1,0:T(8,128)S(1)} %get-tuple-element.9, bf16[256,2,8,128]{0,3,2,1:T(8,128)(2,1)S(1)} %bitcast.163, bf16[256,2,8,128]{0,3,2,1:T(8,128)(2,1)} %bitcast.173, bf16[1024,2,128]{0,2,1:T(8,128)(2,1)S(1)} %bitcast.169), kind=kOutput, calls=%fused_computation.32 | convolution fusion | flops 1084227584 | bytes 10240000 | tf_op jit(solution)/shard_map/rtj,trd->jd/dot_general | solution.py:151
  175.1 1.6 pad_maximum_fusion
  176.7 1.5 copy.130
  178.2 4.4 %all-to-all-start.5 = ((f32[4,256,512]{1,2,0:T(8,128)}), f32[4,256,512]{1,2,0:T(8,128)}, u32[]{:S(2)}, u32[]{:S(2)}) async-start(f32[4,256,512]{1,2,0:T(8,128)} %bitcast.159), calls=%async_computation.5 | async-start | bytes 4194304 | tf_op jit(solution)/shard_map/all_to_all | solution.py:19
  182.6 26.6 %all-to-all-done.5 = f32[4,256,512]{1,2,0:T(8,128)} async-done(((f32[4,256,512]{1,2,0:T(8,128)}), f32[4,256,512]{1,2,0:T(8,128)}, u32[]{:S(2)}, u32[]{:S(2)}) %all-to-all-start.5) | async-done | bytes 2097184 | tf_op jit(solution)/shard_map/all_to_all | solution.py:19
  209.2 1.7 reduce_sum.59
  211.0 9.5 %all_gather.11 = bf16[512,512]{0,1:T(8,128)(2,1)S(1)} all-gather(bf16[512,256]{0,1:T(8,128)(2,1)S(1)} %pad_maximum_fusion.2), channel_id=1, replica_groups=mesh['img'=16,'head'=2,'txt'=4] {'head'}, dimensions={1}, use_global_device_ids=true | all-gather | bytes 786432 | tf_op jit(solution)/shard_map/all_gather | solution.py:60
  220.6 3.5 %fusion.46 = f32[256,3840]{1,0:T(8,128)S(1)} fusion(bf16[3840,512]{1,0:T(8,128)(2,1)} %param.8, bf16[512,512]{0,1:T(8,128)(2,1)S(1)} %all_gather.11), kind=kOutput, calls=%fused_computation.46 | convolution fusion | flops 1006632960 | bytes 8126464 | tf_op jit(solution)/shard_map/dot_general | solution.py:165
  224.1 0.0 copy-done.4
  224.1 2.5 %fusion.12 = bf16[256,3840]{1,0:T(8,128)(2,1)} fusion(f32[256,3840]{1,0:T(8,128)S(1)} %fusion.46, bf16[3840,512]{1,0:T(8,128)(2,1)S(1)} %copy-done.4, bf16[512,512]{0,1:T(8,128)(2,1)S(1)} %all_gather.11), kind=kOutput, calls=%fused_computation.20 | convolution fusion | flops 1008599040 | bytes 10092544 | tf_op jit(solution)/shard_map/dot_general | solution.py:166
  226.6 1.0 copy.134
  227.6 0.0 copy-done.1
  (16 shorter events, 0.2 us)
Async XLA Ops:
  0.6 1.6 copy-start
  0.6 5.0 %copy-start.3 = (bf16[3840,512]{1,0:T(8,128)(2,1)S(1)}, bf16[3840,512]{1,0:T(8,128)(2,1)}, u32[]{:S(2)}) copy-start(bf16[3840,512]{1,0:T(8,128)(2,1)} %param.9) | copy-start | bytes 11796484
  6.8 7.9 %copy-start.7 = (s32[8,8]{1,0:T(8,128)S(1)}, s32[8,8]{1,0:T(8,128)}, u32[]{:S(2)}) copy-start(s32[8,8]{1,0:T(8,128)} %param.13) | copy-start | bytes 772
  6.9 7.9 %copy-start.8 = (s32[8]{0:T(128)S(1)}, s32[8]{0:T(128)}, u32[]{:S(2)}) copy-start(s32[8]{0:T(128)} %param.12) | copy-start | bytes 100
  8.0 20.3 %all-to-all-start = ((f32[2,512,256]{2,1,0:T(8,128)}), f32[2,512,256]{2,1,0:T(8,128)S(1)}, u32[]{:S(2)}, u32[]{:S(2)}) async-start(f32[2,512,256]{2,1,0:T(8,128)} %bitcast.154), calls=%async_computation | async-start | bytes 2097152 | tf_op jit(solution)/shard_map/all_to_all | solution.py:19
  50.6 18.0 %all-to-all-start.1 = ((f32[16,2,8,256]{3,2,1,0:T(8,128)}), f32[16,2,8,256]{3,2,1,0:T(8,128)S(1)}, u32[]{:S(2)}, u32[]{:S(2)}) async-start(f32[16,2,8,256]{3,2,1,0:T(8,128)} %broadcast_in_dim.36), calls=%async_computation.1 | async-start | bytes 524288 | tf_op jit(solution)/shard_map/all_to_all | solution.py:34
  77.3 18.7 %all-to-all-start.3 = ((f32[16,256,16]{1,2,0:T(8,128)}), f32[16,256,16]{1,2,0:T(8,128)S(1)}, u32[]{:S(2)}, u32[]{:S(2)}) async-start(f32[16,256,16]{1,2,0:T(8,128)} %broadcast_in_dim.37), calls=%async_computation.3 | async-start | bytes 524288 | tf_op jit(solution)/shard_map/all_to_all | solution.py:34
  92.9 9.0 %copy-start.2 = (bf16[256,2048]{1,0:T(8,128)(2,1)S(1)}, bf16[256,2048]{1,0:T(8,128)(2,1)}, u32[]{:S(2)}) copy-start(bf16[256,2048]{1,0:T(8,128)(2,1)} %param.11) | copy-start | bytes 3145732
  96.1 33.9 %all-to-all-start.2 = ((f32[16,16,16,128]{3,2,1,0:T(8,128)}), f32[16,16,16,128]{3,2,1,0:T(8,128)}, u32[]{:S(2)}, u32[]{:S(2)}) async-start(f32[16,16,16,128]{3,2,1,0:T(8,128)} %bitcast.158), calls=%async_computation.2 | async-start | bytes 4194304 | tf_op jit(solution)/shard_map/all_to_all | solution.py:19
  132.9 21.0 %all-to-all-start.4 = ((bf16[16,16,2048]{2,1,0:T(8,128)(2,1)}), bf16[16,16,2048]{2,1,0:T(8,128)(2,1)S(1)}, u32[]{:S(2)}, u32[]{:S(2)}) async-start(bf16[16,16,2048]{2,1,0:T(8,128)(2,1)} %broadcast_in_dim.38), calls=%async_computation.4 | async-start | bytes 2097152 | tf_op jit(solution)/shard_map/all_to_all | solution.py:34
  137.5 5.9 %copy-start.5 = (bf16[256,2048]{0,1:T(8,128)(2,1)S(1)}, bf16[256,2048]{0,1:T(8,128)(2,1)}, u32[]{:S(2)}) copy-start(bf16[256,2048]{0,1:T(8,128)(2,1)} %copy.88) | copy-start | bytes 3145732
  167.5 7.6 %copy-start.6 = (f32[1024,128]{0,1:T(8,128)S(1)}, f32[1024,128]{0,1:T(8,128)}, u32[]{:S(2)}) copy-start(f32[1024,128]{0,1:T(8,128)} %fusion.33) | copy-start | bytes 1572868
  178.2 31.1 %all-to-all-start.5 = ((f32[4,256,512]{1,2,0:T(8,128)}), f32[4,256,512]{1,2,0:T(8,128)}, u32[]{:S(2)}, u32[]{:S(2)}) async-start(f32[4,256,512]{1,2,0:T(8,128)} %bitcast.159), calls=%async_computation.5 | async-start | bytes 4194304 | tf_op jit(solution)/shard_map/all_to_all | solution.py:19
  220.5 3.5 %copy-start.4 = (bf16[3840,512]{1,0:T(8,128)(2,1)S(1)}, bf16[3840,512]{1,0:T(8,128)(2,1)}, u32[]{:S(2)}) copy-start(bf16[3840,512]{1,0:T(8,128)(2,1)} %param.9) | copy-start | bytes 11796484
  220.6 7.0 %copy-start.1 = (bf16[256,3840]{1,0:T(8,128)(2,1)S(1)}, bf16[256,3840]{1,0:T(8,128)(2,1)}, u32[]{:S(2)}) copy-start(bf16[256,3840]{1,0:T(8,128)(2,1)} %param.7) | copy-start | bytes 5898244
where the time goes:
time: 229 us; the launch traced here: 228 us
  waiting for transfers between devices  71.3 us (31%)
  matrix products  55 us (24%)
  blocking collectives  36.3 us (16%)
  starting transfers between devices  30.4 us (13%)
  other arithmetic  17.3 us (8%)
  local copies, waits for them, and re-layouts  16.3 us (7%)
    all_to_all x3, waiting for transfers between devices, summed_on_arrival(): lax.all_to_all(in_blocks(array, dim, length), axis, 0, 0, tiled=True)  66.5 us
    all_to_all x3, starting transfers between devices, summed_on_arrival(): lax.all_to_all(in_blocks(array, dim, length), axis, 0, 0, tiled=True)  15.4 us
    dot_general x2, matrix products, shards(): jnp.einsum('rtj,trd->jd', grad_scores, query_heads[:, group_index], prefe...  15.1 us
    all_to_all x3, starting transfers between devices, sent_to_all(): return lax.all_to_all(copies, axis, split_axis=0, concat_axis=0, tiled=True)  15 us
    all_gather x1, blocking collectives, shards(): lax.all_gather(key_own.astype(jnp.bfloat16), 'txt', axis=0, tiled=True)  13.9 us
    all_gather x1, blocking collectives, shards(): lax.all_gather(value_own.astype(jnp.bfloat16), 'txt', axis=0, tiled=True)  12.9 us
    dot_general x2, matrix products, shards(): jnp.einsum('rtj,trd->jd', probabilities.astype(jnp.bfloat16), grad_heads[...  11.6 us
    dot_general x1, matrix products, shards(): jnp.einsum('grtj,jgd->tgrd', weights, value_heads, preferred_element_type...  10 us
  transfers between devices with their start and end apart: 6, of which 4 were waited for; matrix products, arithmetic and copies ran while one was open for 12% of the time, Pallas kernels for 0%

commit v1 on v0

--- a/solution.py
+++ b/solution.py
@@ -7,6 +7,22 @@
 HD = 128
 TILE = 128
 TBLK = 128
+
+
+def gather_around(x, axis, dim):
+    ways, here, lap = (lax.axis_size(axis), lax.axis_index(axis), x.shape[dim])
+    dims = [n * ways if d == dim else n for d, n in enumerate(x.shape)]
+    full = lax.dynamic_update_slice_in_dim(jnp.zeros(dims, x.dtype), x, here * lap, axis=dim)
+    going_up = going_down = x
+    for far in range(1, ways // 2 + 1):
+        going_up = lax.ppermute(going_up, axis, [(d, (d + 1) % ways) for d in range(ways)])
+        full = lax.dynamic_update_slice_in_dim(full, going_up, (here - far) % ways * lap, axis=dim)
+        if 2 * far < ways:
+            going_down = lax.ppermute(going_down, axis, [(d, (d - 1) % ways) for d in range(ways)])
+            full = lax.dynamic_update_slice_in_dim(
+                full, going_down, (here + far) % ways * lap, axis=dim
+            )
+    return full
 
 
 def in_blocks(array, dim, length):
@@ -82,7 +98,7 @@
     value_part = jnp.dot(image_feats, value_weight, preferred_element_type=jnp.float32)
     key_own, value_own = in_one_piece((key_part, value_part), "head", 1, 0)
     keys, values = (
-        lax.all_gather(key_own.astype(jnp.bfloat16), "txt", axis=0, tiled=True),
+        gather_around(key_own.astype(jnp.bfloat16), "txt", 0),
         lax.all_gather(value_own.astype(jnp.bfloat16), "txt", axis=0, tiled=True),
     )
     text_count = queries.shape[0]

time: 229 us -> 228 us (level)
  blocking collectives: 36.3 us -> 22.7 us
  waiting for transfers between devices: 71.3 us -> 80.6 us
  starting transfers between devices: 30.4 us -> 34.7 us
    all_gather x1 -> x0, blocking collectives: 13.9 us -> none  [shards(): lax.all_gather(key_own.astype(jnp.bfloat16), 'txt', axis=0, tiled=True)]
    ppermute x0 -> x3, waiting for transfers between devices: none -> 7.45 us  [the longest x2 6.57 us: gather_around(): lax.ppermute(going_up, axis, [(d, (d + 1) % ways) for d in range(ways)])]
    ppermute x0 -> x3, starting transfers between devices: none -> 3.81 us  [the longest x2 2.08 us: gather_around(): lax.ppermute(going_up, axis, [(d, (d + 1) % ways) for d in range(ways)])]
    unnamed x23 -> x25, local copies, waits for them, and re-layouts: 7.06 us -> 6.13 us
  transfers between devices with their start and end apart: 6 -> 9, of which waited for: 4 -> 7; matrix products, arithmetic and copies ran while one was open for 12% -> 12% of each run, Pallas kernels for 0% -> 0%
where the time goes in v1:
time: 228 us; the launch traced here: 227 us
  waiting for transfers between devices  80.6 us (35%)
  matrix products  55 us (24%)
  starting transfers between devices  34.7 us (15%)
  blocking collectives  22.7 us (10%)
  other arithmetic  17.3 us (8%)
  local copies, waits for them, and re-layouts  15.7 us (7%)
    all_to_all x3, waiting for transfers between devices, summed_on_arrival(): lax.all_to_all(in_blocks(array, dim, length), axis, 0, 0, tiled=True)  68.3 us
    all_to_all x3, starting transfers between devices, sent_to_all(): return lax.all_to_all(copies, axis, split_axis=0, concat_axis=0, tiled=True)  15.5 us
    all_to_all x3, starting transfers between devices, summed_on_arrival(): lax.all_to_all(in_blocks(array, dim, length), axis, 0, 0, tiled=True)  15.4 us
    dot_general x2, matrix products, shards(): jnp.einsum('rtj,trd->jd', grad_scores, query_heads[:, group_index], prefe...  15.1 us
    all_gather x1, blocking collectives, shards(): lax.all_gather(value_own.astype(jnp.bfloat16), 'txt', axis=0, tiled=True)  13.2 us
    dot_general x2, matrix products, shards(): jnp.einsum('rtj,trd->jd', probabilities.astype(jnp.bfloat16), grad_heads[...  11.6 us
    dot_general x1, matrix products, shards(): jnp.einsum('grtj,jgd->tgrd', weights, value_heads, preferred_element_type...  10 us
    all_gather x1, blocking collectives, side_by_side(): out = lax.all_gather(both, axis, axis=dim, tiled=True)  9.52 us
  transfers between devices with their start and end apart: 9, of which 7 were waited for; matrix products, arithmetic and copies ran while one was open for 12% of the time, Pallas kernels for 0%

profile of v1, /device:TPU:0, one launch (start us, length us, event | category | flops | bytes accessed | tf_op | source)
XLA Modules:
  0.0 227.1 jit_solution(4943375516449773845)
XLA Ops:
  0.6 0.0 copy-start
  0.6 0.0 copy-start.3
  0.7 1.5 copy-done
  2.2 3.5 %fusion.59 = f32[256,512]{1,0:T(8,128)S(1)} fusion(bf16[256,3840]{1,0:T(8,128)(2,1)S(1)} %copy-done, bf16[3840,512]{1,0:T(8,128)(2,1)} %param.8), kind=kOutput, calls=%fused_computation.76 | convolution fusion | flops 1006632960 | bytes 6422528 | tf_op jit(solution)/shard_map/dot_general | solution.py:97
  5.7 1.2 fusion.60
  6.8 0.0 copy-start.8
  6.9 0.1 pad_maximum_fusion.1
  7.0 1.1 copy.140
  8.0 5.2 %all-to-all-start = ((f32[2,512,256]{2,1,0:T(8,128)}), f32[2,512,256]{2,1,0:T(8,128)S(1)}, u32[]{:S(2)}, u32[]{:S(2)}) async-start(f32[2,512,256]{2,1,0:T(8,128)} %bitcast.154), calls=%async_computation | async-start | bytes 2097152 | tf_op jit(solution)/shard_map/all_to_all | solution.py:35
  13.3 15.1 %all-to-all-done = f32[2,512,256]{2,1,0:T(8,128)S(1)} async-done(((f32[2,512,256]{2,1,0:T(8,128)}), f32[2,512,256]{2,1,0:T(8,128)S(1)}, u32[]{:S(2)}, u32[]{:S(2)}) %all-to-all-start) | async-done | bytes 1048608 | tf_op jit(solution)/shard_map/all_to_all | solution.py:35
  28.3 0.1 reduce_sum.54
  28.4 1.6 collective-permute-start
  30.1 0.3 fusion.42
  30.4 0.5 copy.91
  31.0 0.1 copy.87
  31.1 1.7 collective-permute-start.1
  32.8 0.1 broadcast_in_dim.38
  32.9 1.8 collective-permute-done
  34.7 0.1 copy.88
  34.8 0.4 collective-permute-start.2
  35.2 0.9 collective-permute-done.1
  36.1 0.1 copy.89
  36.3 4.8 %collective-permute-done.2 = bf16[256,256]{1,0:T(8,128)(2,1)S(1)} collective-permute-done((bf16[256,256]{1,0:T(8,128)(2,1)S(1)}, bf16[256,256]{1,0:T(8,128)(2,1)S(1)}, u32[]{:S(2)}, u32[]{:S(2)}) %collective-permute-start.2) | collective-permute-done | bytes 131104 | tf_op jit(solution)/shard_map/ppermute | solution.py:18
  41.0 0.1 copy.90
  41.2 0.1 broadcast_in_dim.35
  41.3 7.3 %fusion.58 = (f32[2,8,256]{2,1,0:T(8,128)S(1)}, f32[2,8,256,1024]{2,3,1,0:T(8,128)}) fusion(bf16[1024,2,128,1]{0,2,3,1:T(8,128)(2,1)S(1)} %bitcast.166, bf16[256,2,8,128]{0,3,2,1:T(8,128)(2,1)S(1)} %bitcast.161, pred[256,1024]{0,1:T(8,128)(4,1)S(1)} %bitcast.164), kind=kOutput, calls=%fused_computation.75 | convolution fusion | flops 1086320640 | bytes 18628608 | tf_op jit(solution)/shard_map/tgrd,jgd->grtj/dot_general | solution.py:115
  48.5 0.7 broadcast_in_dim.40
  49.2 4.9 %all-to-all-start.1 = ((f32[16,2,8,256]{3,2,1,0:T(8,128)}), f32[16,2,8,256]{3,2,1,0:T(8,128)S(1)}, u32[]{:S(2)}, u32[]{:S(2)}) async-start(f32[16,2,8,256]{3,2,1,0:T(8,128)} %broadcast_in_dim.40), calls=%async_computation.1 | async-start | bytes 524288 | tf_op jit(solution)/shard_map/all_to_all | solution.py:50
  54.1 13.2 %all_gather.6 = bf16[1024,256]{1,0:T(8,128)(2,1)S(1)} all-gather(bf16[256,256]{1,0:T(8,128)(2,1)S(1)} %get-tuple-element.7), channel_id=1, replica_groups=mesh['img'=16,'head'=2,'txt'=4] {'txt'}, dimensions={0}, use_global_device_ids=true | all-gather | bytes 655360 | tf_op jit(solution)/shard_map/all_gather | solution.py:102
  67.3 0.2 copy.86
  67.6 8.0 %convert_reduce_fusion = f32[2,8,256]{2,1,0:T(8,128)S(1)} fusion(f32[2,8,256,1024]{2,3,1,0:T(8,128)} %get-tuple-element.11, f32[2,8,256]{2,1,0:T(8,128)S(1)} %reduce_max.19), kind=kLoop, calls=%fused_computation.1 | loop fusion | flops 16773120 | bytes 16809984 | tf_op jit(solution)/shard_map/reduce_sum | solution.py:122
  75.5 0.7 broadcast_in_dim.41
  76.3 5.9 %all-to-all-start.3 = ((f32[16,256,16]{1,2,0:T(8,128)}), f32[16,256,16]{1,2,0:T(8,128)S(1)}, u32[]{:S(2)}, u32[]{:S(2)}) async-start(f32[16,256,16]{1,2,0:T(8,128)} %broadcast_in_dim.41), calls=%async_computation.3 | async-start | bytes 524288 | tf_op jit(solution)/shard_map/all_to_all | solution.py:50
  82.2 10.0 %fusion.26 = f32[256,2,8,128]{0,3,2,1:T(8,128)} fusion(bf16[1024,2,128,1]{0,2,3,1:T(8,128)(2,1)S(1)} %bitcast.167, f32[2,8,256,1024]{2,3,1,0:T(8,128)} %get-tuple-element.11, f32[2,8,256]{2,1,0:T(8,128)S(1)} %reduce_max.19), kind=kOutput, calls=%fused_computation.31 | convolution fusion | flops 1082130432 | bytes 19415040 | tf_op jit(solution)/shard_map/grtj,jgd->tgrd/dot_general | solution.py:126
  92.2 3.2 %copy.95 = f32[256,2,8,128]{3,2,1,0:T(8,128)} copy(f32[256,2,8,128]{0,3,2,1:T(8,128)} %fusion.26) | data formatting | bytes 4194304 | tf_op jit(solution)/shard_map/grtj,jgd->tgrd/transpose | solution.py:126
  95.4 5.8 %all-to-all-start.2 = ((f32[16,16,16,128]{3,2,1,0:T(8,128)}), f32[16,16,16,128]{3,2,1,0:T(8,128)}, u32[]{:S(2)}, u32[]{:S(2)}) async-start(f32[16,16,16,128]{3,2,1,0:T(8,128)} %bitcast.158), calls=%async_computation.2 | async-start | bytes 4194304 | tf_op jit(solution)/shard_map/all_to_all | solution.py:35
  101.2 1.3 copy.97
  102.5 0.1 constant_dynamic-slice_fusion
  102.6 0.1 copy.96
  102.7 26.6 %all-to-all-done.2 = f32[16,16,16,128]{3,2,1,0:T(8,128)} async-done(((f32[16,16,16,128]{3,2,1,0:T(8,128)}), f32[16,16,16,128]{3,2,1,0:T(8,128)}, u32[]{:S(2)}, u32[]{:S(2)}) %all-to-all-start.2) | async-done | bytes 2097184 | tf_op jit(solution)/shard_map/all_to_all | solution.py:35
  129.3 1.7 reduce_sum.55
  131.0 0.1 divide_convert_fusion
  131.1 1.1 broadcast_in_dim.42
  132.2 4.7 %all-to-all-start.4 = ((bf16[16,16,2048]{2,1,0:T(8,128)(2,1)}), bf16[16,16,2048]{2,1,0:T(8,128)(2,1)S(1)}, u32[]{:S(2)}, u32[]{:S(2)}) async-start(bf16[16,16,2048]{2,1,0:T(8,128)(2,1)} %broadcast_in_dim.42), calls=%async_computation.4 | async-start | bytes 2097152 | tf_op jit(solution)/shard_map/all_to_all | solution.py:50
  137.0 5.9 %fusion.33 = f32[1024,128]{0,1:T(8,128)} fusion(f32[2,8,256,1024]{2,3,1,0:T(8,128)} %get-tuple-element.11, f32[8,256]{1,0:T(8,128)S(1)} %get-tuple-element.8, bf16[256,2,8,128]{0,3,2,1:T(8,128)(2,1)} %bitcast.171), kind=kOutput, calls=%fused_computation.34 | convolution fusion | flops 541065216 | bytes 9445376 | tf_op jit(solution)/shard_map/rtj,trd->jd/dot_general | solution.py:159
  142.9 5.7 %fusion.36 = f32[1024,128]{0,1:T(8,128)} fusion(f32[2,8,256,1024]{2,3,1,0:T(8,128)} %get-tuple-element.11, f32[8,256]{1,0:T(8,128)S(1)} %get-tuple-element.9, bf16[256,2,8,128]{0,3,2,1:T(8,128)(2,1)S(1)} %bitcast.174), kind=kOutput, calls=%fused_computation.35 | convolution fusion | flops 541065216 | bytes 9445376 | tf_op jit(solution)/shard_map/rtj,trd->jd/dot_general | solution.py:159
  148.6 4.9 %all-to-all-done.4 = bf16[16,16,2048]{2,1,0:T(8,128)(2,1)S(1)} async-done(((bf16[16,16,2048]{2,1,0:T(8,128)(2,1)}), bf16[16,16,2048]{2,1,0:T(8,128)(2,1)S(1)}, u32[]{:S(2)}, u32[]{:S(2)}) %all-to-all-start.4) | async-done | bytes 1048608 | tf_op jit(solution)/shard_map/all_to_all | solution.py:50
  153.5 1.6 multiply_bitcast_fusion
  155.0 1.7 copy.135
  156.8 2.4 %reduce_sum.58 = f32[256,2,8]{2,1,0:T(2,128)S(1)} reduce(f32[256,2,8,128]{3,2,1,0:T(8,128)} %bitcast.157, f32[]{:T(128)} %constant.51.clone.1), dimensions={3}, to_apply=%region_6.7 | reduce | flops 520192 | bytes 2113540 | tf_op jit(solution)/shard_map/reduce_sum | solution.py:142
  159.1 0.2 fusion.56
  159.4 0.1 copy.100
  159.4 0.1 copy.104
  159.5 7.6 %fusion.30 = f32[1024,128]{0,1:T(8,128)} fusion(f32[2,8,256,1024]{2,3,1,0:T(8,128)} %get-tuple-element.11, f32[8,256]{1,0:T(8,128)S(1)} %copy.100, f32[8,256]{1,0:T(8,128)S(1)} %get-tuple-element.8, bf16[256,2,8,128]{0,3,2,1:T(8,128)(2,1)S(1)} %bitcast.162, bf16[256,2,8,128]{0,3,2,1:T(8,128)(2,1)} %bitcast.172, bf16[1024,2,128]{0,2,1:T(8,128)(2,1)S(1)} %bitcast.168), kind=kOutput, calls=%fused_computation.33 | convolution fusion | flops 1084227584 | bytes 10240000 | tf_op jit(solution)/shard_map/rtj,trd->jd/dot_general | solution.py:167
  167.0 7.6 %fusion.27 = f32[1024,128]{0,1:T(8,128)} fusion(f32[2,8,256,1024]{2,3,1,0:T(8,128)} %get-tuple-element.11, f32[8,256]{1,0:T(8,128)S(1)} %copy.104, f32[8,256]{1,0:T(8,128)S(1)} %get-tuple-element.9, bf16[256,2,8,128]{0,3,2,1:T(8,128)(2,1)S(1)} %bitcast.163, bf16[256,2,8,128]{0,3,2,1:T(8,128)(2,1)} %bitcast.173, bf16[1024,2,128]{0,2,1:T(8,128)(2,1)S(1)} %bitcast.169), kind=kOutput, calls=%fused_computation.32 | convolution fusion | flops 1084227584 | bytes 10240000 | tf_op jit(solution)/shard_map/rtj,trd->jd/dot_general | solution.py:167
  174.6 1.6 pad_maximum_fusion
  176.2 1.5 copy.139
  177.7 4.4 %all-to-all-start.5 = ((f32[4,256,512]{1,2,0:T(8,128)}), f32[4,256,512]{1,2,0:T(8,128)}, u32[]{:S(2)}, u32[]{:S(2)}) async-start(f32[4,256,512]{1,2,0:T(8,128)} %bitcast.159), calls=%async_computation.5 | async-start | bytes 4194304 | tf_op jit(solution)/shard_map/all_to_all | solution.py:35
  182.1 26.6 %all-to-all-done.5 = f32[4,256,512]{1,2,0:T(8,128)} async-done(((f32[4,256,512]{1,2,0:T(8,128)}), f32[4,256,512]{1,2,0:T(8,128)}, u32[]{:S(2)}, u32[]{:S(2)}) %all-to-all-start.5) | async-done | bytes 2097184 | tf_op jit(solution)/shard_map/all_to_all | solution.py:35
  208.7 1.7 reduce_sum.59
  210.5 9.5 %all_gather.7 = bf16[512,512]{0,1:T(8,128)(2,1)S(1)} all-gather(bf16[512,256]{0,1:T(8,128)(2,1)S(1)} %pad_maximum_fusion.2), channel_id=1, replica_groups=mesh['img'=16,'head'=2,'txt'=4] {'head'}, dimensions={1}, use_global_device_ids=true | all-gather | bytes 786432 | tf_op jit(solution)/shard_map/all_gather | solution.py:76
  220.1 3.5 %fusion.46 = f32[256,3840]{1,0:T(8,128)S(1)} fusion(bf16[3840,512]{1,0:T(8,128)(2,1)} %param.8, bf16[512,512]{0,1:T(8,128)(2,1)S(1)} %all_gather.7), kind=kOutput, calls=%fused_computation.46 | convolution fusion | flops 1006632960 | bytes 8126464 | tf_op jit(solution)/shard_map/dot_general | solution.py:181
  223.6 2.5 %fusion.12 = bf16[256,3840]{1,0:T(8,128)(2,1)} fusion(f32[256,3840]{1,0:T(8,128)S(1)} %fusion.46, bf16[3840,512]{1,0:T(8,128)(2,1)S(1)} %copy-done.4, bf16[512,512]{0,1:T(8,128)(2,1)S(1)} %all_gather.7), kind=kOutput, calls=%fused_computation.20 | convolution fusion | flops 1008599040 | bytes 10092544 | tf_op jit(solution)/shard_map/dot_general | solution.py:182
  226.1 1.0 copy.147
  (31 shorter events, 0.3 us)
Async XLA Ops:
  0.6 1.6 copy-start
  0.6 5.0 %copy-start.3 = (bf16[3840,512]{1,0:T(8,128)(2,1)S(1)}, bf16[3840,512]{1,0:T(8,128)(2,1)}, u32[]{:S(2)}) copy-start(bf16[3840,512]{1,0:T(8,128)(2,1)} %param.9) | copy-start | bytes 11796484
  6.8 23.2 %copy-start.8 = (s32[8,8]{1,0:T(8,128)S(1)}, s32[8,8]{1,0:T(8,128)}, u32[]{:S(2)}) copy-start(s32[8,8]{1,0:T(8,128)} %param.13) | copy-start | bytes 772
  6.9 23.2 %copy-start.9 = (s32[8]{0:T(128)S(1)}, s32[8]{0:T(128)}, u32[]{:S(2)}) copy-start(s32[8]{0:T(128)} %param.12) | copy-start | bytes 100
  6.9 23.6 %copy-start.5 = (bf16[256,2048]{1,0:T(8,128)(2,1)S(1)}, bf16[256,2048]{1,0:T(8,128)(2,1)}, u32[]{:S(2)}) copy-start(bf16[256,2048]{1,0:T(8,128)(2,1)} %param.10) | copy-start | bytes 3145732
  8.0 20.3 %all-to-all-start = ((f32[2,512,256]{2,1,0:T(8,128)}), f32[2,512,256]{2,1,0:T(8,128)S(1)}, u32[]{:S(2)}, u32[]{:S(2)}) async-start(f32[2,512,256]{2,1,0:T(8,128)} %bitcast.154), calls=%async_computation | async-start | bytes 2097152 | tf_op jit(solution)/shard_map/all_to_all | solution.py:35
  28.4 6.2 %collective-permute-start = (bf16[256,256]{1,0:T(8,128)(2,1)S(1)}, bf16[256,256]{1,0:T(8,128)(2,1)S(1)}, u32[]{:S(2)}, u32[]{:S(2)}) collective-permute-start(bf16[256,256]{1,0:T(8,128)(2,1)S(1)} %get-tuple-element.6), channel_id=1, source_target_pairs={{0,1},{1,2},{2,3},{3,0},{4,5},{5,6},{6,7},{7,4},{8,9},{9,10},{10,1... | collective-permute-start | bytes 393224 | tf_op jit(solution)/shard_map/ppermute | solution.py:18
  31.1 5.0 %collective-permute-start.1 = (bf16[256,256]{1,0:T(8,128)(2,1)S(1)}, bf16[256,256]{1,0:T(8,128)(2,1)S(1)}, u32[]{:S(2)}, u32[]{:S(2)}) collective-permute-start(bf16[256,256]{1,0:T(8,128)(2,1)S(1)} %get-tuple-element.6), channel_id=1, source_target_pairs={{0,3},{1,0},{2,1},{3,2},{4,7},{5,4},{6,5},{7,6},{8,11},{9,8},{10,9... | collective-permute-start | bytes 393224 | tf_op jit(solution)/shard_map/ppermute | solution.py:21
  34.8 6.2 %collective-permute-start.2 = (bf16[256,256]{1,0:T(8,128)(2,1)S(1)}, bf16[256,256]{1,0:T(8,128)(2,1)S(1)}, u32[]{:S(2)}, u32[]{:S(2)}) collective-permute-start(bf16[256,256]{1,0:T(8,128)(2,1)S(1)} %collective-permute-done), channel_id=1, source_target_pairs={{0,1},{1,2},{2,3},{3,0},{4,5},{5,6},{6,7},{7,4},{8,9},{9,10},{10,1... | collective-permute-start | bytes 393224 | tf_op jit(solution)/shard_map/ppermute | solution.py:18
  49.2 18.3 %all-to-all-start.1 = ((f32[16,2,8,256]{3,2,1,0:T(8,128)}), f32[16,2,8,256]{3,2,1,0:T(8,128)S(1)}, u32[]{:S(2)}, u32[]{:S(2)}) async-start(f32[16,2,8,256]{3,2,1,0:T(8,128)} %broadcast_in_dim.40), calls=%async_computation.1 | async-start | bytes 524288 | tf_op jit(solution)/shard_map/all_to_all | solution.py:50
  76.3 19.1 %all-to-all-start.3 = ((f32[16,256,16]{1,2,0:T(8,128)}), f32[16,256,16]{1,2,0:T(8,128)S(1)}, u32[]{:S(2)}, u32[]{:S(2)}) async-start(f32[16,256,16]{1,2,0:T(8,128)} %broadcast_in_dim.41), calls=%async_computation.3 | async-start | bytes 524288 | tf_op jit(solution)/shard_map/all_to_all | solution.py:50
  92.2 9.0 %copy-start.2 = (bf16[256,2048]{1,0:T(8,128)(2,1)S(1)}, bf16[256,2048]{1,0:T(8,128)(2,1)}, u32[]{:S(2)}) copy-start(bf16[256,2048]{1,0:T(8,128)(2,1)} %param.11) | copy-start | bytes 3145732
  95.4 33.9 %all-to-all-start.2 = ((f32[16,16,16,128]{3,2,1,0:T(8,128)}), f32[16,16,16,128]{3,2,1,0:T(8,128)}, u32[]{:S(2)}, u32[]{:S(2)}) async-start(f32[16,16,16,128]{3,2,1,0:T(8,128)} %bitcast.158), calls=%async_computation.2 | async-start | bytes 4194304 | tf_op jit(solution)/shard_map/all_to_all | solution.py:35
  132.2 21.2 %all-to-all-start.4 = ((bf16[16,16,2048]{2,1,0:T(8,128)(2,1)}), bf16[16,16,2048]{2,1,0:T(8,128)(2,1)S(1)}, u32[]{:S(2)}, u32[]{:S(2)}) async-start(bf16[16,16,2048]{2,1,0:T(8,128)(2,1)} %broadcast_in_dim.42), calls=%async_computation.4 | async-start | bytes 2097152 | tf_op jit(solution)/shard_map/all_to_all | solution.py:50
  137.0 5.9 %copy-start.6 = (bf16[256,2048]{0,1:T(8,128)(2,1)S(1)}, bf16[256,2048]{0,1:T(8,128)(2,1)}, u32[]{:S(2)}) copy-start(bf16[256,2048]{0,1:T(8,128)(2,1)} %copy.97) | copy-start | bytes 3145732
  167.0 7.6 %copy-start.7 = (f32[1024,128]{0,1:T(8,128)S(1)}, f32[1024,128]{0,1:T(8,128)}, u32[]{:S(2)}) copy-start(f32[1024,128]{0,1:T(8,128)} %fusion.33) | copy-start | bytes 1572868
  177.7 31.1 %all-to-all-start.5 = ((f32[4,256,512]{1,2,0:T(8,128)}), f32[4,256,512]{1,2,0:T(8,128)}, u32[]{:S(2)}, u32[]{:S(2)}) async-start(f32[4,256,512]{1,2,0:T(8,128)} %bitcast.159), calls=%async_computation.5 | async-start | bytes 4194304 | tf_op jit(solution)/shard_map/all_to_all | solution.py:35
  220.0 3.5 %copy-start.4 = (bf16[3840,512]{1,0:T(8,128)(2,1)S(1)}, bf16[3840,512]{1,0:T(8,128)(2,1)}, u32[]{:S(2)}) copy-start(bf16[3840,512]{1,0:T(8,128)(2,1)} %param.9) | copy-start | bytes 11796484
  220.0 7.0 %copy-start.1 = (bf16[256,3840]{1,0:T(8,128)(2,1)S(1)}, bf16[256,3840]{1,0:T(8,128)(2,1)}, u32[]{:S(2)}) copy-start(bf16[256,3840]{1,0:T(8,128)(2,1)} %param.7) | copy-start | bytes 5898244
